TPU v7x, 128 devices: a whole 4x4x4 slice. The times are simulated.
128 devices in a mesh: fsdp: 4 (over y_lo, core), ctx: 32 (over z, y_hi, x).
Axes of the slice: x: 4, y: 4 (y_hi: 2, y_lo: 2; y = y_hi * 2 + y_lo), z: 4, core: 2. Of those that a mesh axis runs over, the one named last changes fastest.
Arguments:
- query_proj: bfloat16 [4, 4096, 4096], P('fsdp', 'ctx'), may hold values from -10 to 10
- key_proj: bfloat16 [4, 4096, 4096], P('fsdp', 'ctx'), may hold values from -10 to 10
- value_proj: bfloat16 [4, 4096, 4096], P('fsdp', 'ctx'), may hold values from -12 to 12
- modality: int32 [4, 4096], P('fsdp', 'ctx'), may hold values from 0 to 1, as said below
- out_weight: bfloat16 [2, 4096, 2048], P(None, ('fsdp', 'ctx')), may hold values from -0.09375 to 0.09375
- grad_projected: bfloat16 [4, 4096, 2048], P('fsdp', 'ctx'), may hold values from -6 to 6
Outputs:
- projected: bfloat16 [4, 4096, 2048], P('fsdp', 'ctx')
- grad_query: bfloat16 [4, 4096, 4096], P('fsdp', 'ctx')
- grad_key: bfloat16 [4, 4096, 4096], P('fsdp', 'ctx')
- grad_value: bfloat16 [4, 4096, 4096], P('fsdp', 'ctx')
Inputs may be any that keep to these rules, and one draw needn't show every extreme that they name: `modality`: each sequence holds exactly two image spans of 1024 positions each, one starting within the first half and lying in the first half, the other lying in the second half; all other positions are text, so exactly half of each sequence's positions are image.
All inputs are finite; a program needn't handle non-finite values.
Results may differ from a plain program's by a relative error of at most 0.012.
The roundings to bfloat16 on the way count: a program that leaves them out, or rounds other values in their place, can miss the bound.
Values may be sent and summed in bfloat16 or wider, within the bound.
No kernel may reach another device: no remote copies, remote signals or barrier semaphores. Data moves between devices by JAX's collectives and lax.ppermute only.
A program may use at most 320 MiB of HBM per device.

v0:
```python
import jax
import jax.numpy as jnp
from jax import lax
from jax.sharding import PartitionSpec as P

HEAD_SIZE = 128


def cut_along(array, dim, length):
    before, after = (array.shape[:dim], array.shape[dim + 1 :])
    return jnp.moveaxis(array.reshape(*before, length, -1, *after), dim, 0)


def edges_of(length, count):
    unit = 8 if length >= 8 * count else 1
    return [length // unit * k // count * unit for k in range(1, count)]


def in_order(blocks, dim):
    dims = list(blocks.shape[1:])
    dims[dim] *= blocks.shape[0]
    return jnp.moveaxis(blocks, 0, dim).reshape(dims)


def exchange_in_pieces(array, axis, pieces, split_dim, concat_dim):
    blocks = cut_along(array, split_dim, lax.axis_size(axis))
    widest = max(range(1, max(2, blocks.ndim - 1)), key=lambda d: blocks.shape[d])
    done = []
    for share in jnp.split(blocks, edges_of(blocks.shape[widest], pieces), axis=widest):
        if share.size:
            done.append(lax.all_to_all(share, axis, split_axis=0, concat_axis=0, tiled=True))
    return in_order(jnp.concatenate(done, axis=widest), concat_dim)


def sent_together(arrays, axis, split_dim, concat_dim, along):
    widths = [a.shape[along] for a in arrays]
    both = jnp.concatenate(arrays, axis=along)
    filled = lax.all_to_all(both, axis, split_axis=split_dim, concat_axis=concat_dim, tiled=True)
    return tuple(jnp.split(filled, [sum(widths[:k]) for k in range(1, len(widths))], axis=along))


def block_count(length):
    return max(1, min(8, length // 512))


def probabilities(query_block, key_prefix, offset):
    scaling = query_block.shape[-1] ** (-0.5)
    scores = (
        jnp.einsum("hqd,hkd->hqk", query_block, key_prefix, preferred_element_type=jnp.float32)
        * scaling
    )
    query_places = offset + jnp.arange(query_block.shape[1])
    key_places = jnp.arange(key_prefix.shape[1])
    scores = jnp.where(key_places[None, None, :] <= query_places[None, :, None], scores, -jnp.inf)
    highest = jnp.max(scores, axis=-1, keepdims=True)
    raised = jnp.exp(scores - highest)
    return raised / jnp.sum(raised, axis=-1, keepdims=True)


def attend_forward(queries, keys_all, values_all):
    length = queries.shape[1]
    block_rows = length // block_count(length)
    pieces = []
    for block_index in range(length // block_rows):
        offset = block_index * block_rows
        finish = offset + block_rows
        weights = probabilities(queries[:, offset:finish], keys_all[:, :finish], offset).astype(
            jnp.bfloat16
        )
        output = jnp.einsum(
            "hqk,hkd->hqd", weights, values_all[:, :finish], preferred_element_type=jnp.float32
        )
        pieces.append(output.astype(jnp.bfloat16))
    return jnp.concatenate(pieces, axis=1)


def attend_backward(queries, keys_all, values_all, attention, grad_attention):
    length = queries.shape[1]
    block_rows = length // block_count(length)
    scaling = queries.shape[-1] ** (-0.5)
    grad_keys = jnp.zeros(queries.shape, jnp.float32)
    grad_values = jnp.zeros(queries.shape, jnp.float32)
    query_pieces = []
    for block_index in range(length // block_rows):
        offset = block_index * block_rows
        finish = offset + block_rows
        query_block = queries[:, offset:finish]
        weights = probabilities(query_block, keys_all[:, :finish], offset)
        grad_block = grad_attention[:, offset:finish]
        attn_block = attention[:, offset:finish]
        grad_values = grad_values.at[:, :finish].add(
            jnp.einsum(
                "hqk,hqd->hkd",
                weights.astype(jnp.bfloat16),
                grad_block,
                preferred_element_type=jnp.float32,
            )
        )
        grad_weights = jnp.einsum(
            "hqd,hkd->hqk", grad_block, values_all[:, :finish], preferred_element_type=jnp.float32
        )
        row_delta = jnp.sum(
            grad_block.astype(jnp.float32) * attn_block.astype(jnp.float32), axis=-1, keepdims=True
        )
        grad_scores = (weights * (grad_weights - row_delta) * scaling).astype(jnp.bfloat16)
        query_pieces.append(
            jnp.einsum(
                "hqk,hkd->hqd",
                grad_scores,
                keys_all[:, :finish],
                preferred_element_type=jnp.float32,
            ).astype(jnp.bfloat16)
        )
        grad_keys = grad_keys.at[:, :finish].add(
            jnp.einsum("hqk,hqd->hkd", grad_scores, query_block, preferred_element_type=jnp.float32)
        )
    return (
        jnp.concatenate(query_pieces, axis=1),
        grad_keys.astype(jnp.bfloat16),
        grad_values.astype(jnp.bfloat16),
    )


def transposed_product(left, right):
    return lax.dot_general(
        left, right, (((1,), (1,)), ((), ())), preferred_element_type=jnp.float32
    )


def heads_first(flat, length, local_heads):
    return flat.reshape(length, local_heads, HEAD_SIZE).transpose(1, 0, 2)


def heads_last(stacked, length, local_width):
    return stacked.transpose(1, 0, 2).reshape(1, length, local_width)


def per_device(query_proj, key_proj, value_proj, modality, out_weight, grad_projected):
    context_size = lax.axis_size("ctx")
    row_count = query_proj.shape[1]
    inner_width = query_proj.shape[2]
    length = row_count * context_size
    local_width = inner_width // context_size
    local_heads = local_width // HEAD_SIZE
    head_query, head_key, head_value = (
        exchange_in_pieces(query_proj, "ctx", 2, 2, 1),
        exchange_in_pieces(key_proj, "ctx", 2, 2, 1),
        exchange_in_pieces(value_proj, "ctx", 2, 2, 1),
    )
    head_query = heads_first(head_query, length, local_heads)
    head_key = heads_first(head_key, length, local_heads)
    head_value = heads_first(head_value, length, local_heads)
    attention = attend_forward(head_query, head_key, head_value)
    sending = heads_last(attention, length, local_width)
    attn_rows = lax.all_to_all(sending, "ctx", split_axis=1, concat_axis=2, tiled=True)[0]
    upstream = grad_projected[0]
    weight_piece = lax.all_gather(out_weight, ("fsdp", "ctx"), axis=1, tiled=True)
    text_out = jnp.dot(attn_rows, weight_piece[0], preferred_element_type=jnp.float32)
    image_out = jnp.dot(attn_rows, weight_piece[1], preferred_element_type=jnp.float32)
    text_grad = transposed_product(upstream, weight_piece[0])
    image_grad = transposed_product(upstream, weight_piece[1])
    text_out, image_out, text_grad, image_grad = (text_out, image_out, text_grad, image_grad)
    image_rows = (modality[0] == 1)[:, None]
    projected = jnp.where(image_rows, image_out, text_out).astype(jnp.bfloat16)[None]
    grad_rows = jnp.where(image_rows, image_grad, text_grad).astype(jnp.bfloat16)
    grad_heads = lax.all_to_all(grad_rows[None], "ctx", split_axis=2, concat_axis=1, tiled=True)
    grad_heads = heads_first(grad_heads, length, local_heads)
    grad_q, grad_k, grad_v = attend_backward(
        head_query, head_key, head_value, attention, grad_heads
    )
    grad_query, grad_key, grad_value = sent_together(
        (
            heads_last(grad_q, length, local_width),
            heads_last(grad_k, length, local_width),
            heads_last(grad_v, length, local_width),
        ),
        "ctx",
        1,
        2,
        0,
    )
    return (projected, grad_query, grad_key, grad_value)


def solution(mesh):
    placed = (
        P("fsdp", "ctx", None),
        P("fsdp", "ctx", None),
        P("fsdp", "ctx", None),
        P("fsdp", "ctx"),
        P(None, ("fsdp", "ctx"), None),
        P("fsdp", "ctx", None),
    )
    return jax.shard_map(
        per_device,
        mesh=mesh,
        in_specs=placed,
        out_specs=(
            P("fsdp", "ctx", None),
            P("fsdp", "ctx", None),
            P("fsdp", "ctx", None),
            P("fsdp", "ctx", None),
        ),
        check_vma=False,
    )
```

profile of v0, /device:TPU:18, one launch (start us, length us, event | category | flops | bytes accessed | tf_op | source)
XLA Modules:
  0.0 680.0 jit_solution(4088822224911274134)
XLA Ops:
  13.4 10.9 %all-to-all-start.3 = ((bf16[32,1,64,128]{3,2,1,0:T(8,128)(2,1)}), bf16[32,1,64,128]{3,2,1,0:T(8,128)(2,1)S(1)}, u32[]{:S(2)}, u32[]{:S(2)}) async-start(bf16[32,1,64,128]{3,2,1,0:T(8,128)(2,1)} %copy.65), calls=%async_computation.3 | async-start | bytes 1048576 | tf_op jit(solution)/shard_map/all_to_all | solution.py:31
  25.4 11.5 %all-to-all-done.3 = bf16[32,1,64,128]{3,2,1,0:T(8,128)(2,1)S(1)} async-done(((bf16[32,1,64,128]{3,2,1,0:T(8,128)(2,1)}), bf16[32,1,64,128]{3,2,1,0:T(8,128)(2,1)S(1)}, u32[]{:S(2)}, u32[]{:S(2)}) %all-to-all-start.3) | async-done | bytes 524320 | tf_op jit(solution)/shard_map/all_to_all | solution.py:31
  36.8 7.5 %all-to-all-start.2 = ((bf16[32,1,64,128]{3,2,1,0:T(8,128)(2,1)}), bf16[32,1,64,128]{3,2,1,0:T(8,128)(2,1)}, u32[]{:S(2)}, u32[]{:S(2)}) async-start(bf16[32,1,64,128]{3,2,1,0:T(8,128)(2,1)} %copy.64), calls=%async_computation.2 | async-start | bytes 1048576 | tf_op jit(solution)/shard_map/all_to_all | solution.py:31
  49.7 6.4 all-to-all-done.2
  56.1 7.5 %all-to-all-start.1 = ((bf16[32,1,64,128]{3,2,1,0:T(8,128)(2,1)}), bf16[32,1,64,128]{3,2,1,0:T(8,128)(2,1)S(1)}, u32[]{:S(2)}, u32[]{:S(2)}) async-start(bf16[32,1,64,128]{3,2,1,0:T(8,128)(2,1)} %copy.60), calls=%async_computation.1 | async-start | bytes 1048576 | tf_op jit(solution)/shard_map/all_to_all | solution.py:31
  64.8 10.1 %all-to-all-done.1 = bf16[32,1,64,128]{3,2,1,0:T(8,128)(2,1)S(1)} async-done(((bf16[32,1,64,128]{3,2,1,0:T(8,128)(2,1)}), bf16[32,1,64,128]{3,2,1,0:T(8,128)(2,1)S(1)}, u32[]{:S(2)}, u32[]{:S(2)}) %all-to-all-start.1) | async-done | bytes 524320 | tf_op jit(solution)/shard_map/all_to_all | solution.py:31
  75.7 7.6 %all-to-all-start = ((bf16[32,1,64,128]{3,2,1,0:T(8,128)(2,1)}), bf16[32,1,64,128]{3,2,1,0:T(8,128)(2,1)}, u32[]{:S(2)}, u32[]{:S(2)}) async-start(bf16[32,1,64,128]{3,2,1,0:T(8,128)(2,1)} %copy.59), calls=%async_computation | async-start | bytes 1048576 | tf_op jit(solution)/shard_map/all_to_all | solution.py:31
  92.8 7.9 %all-to-all-start.5 = ((bf16[32,1,64,128]{3,2,1,0:T(8,128)(2,1)}), bf16[32,1,64,128]{3,2,1,0:T(8,128)(2,1)S(1)}, u32[]{:S(2)}, u32[]{:S(2)}) async-start(bf16[32,1,64,128]{3,2,1,0:T(8,128)(2,1)} %copy.70), calls=%async_computation.5 | async-start | bytes 1048576 | tf_op jit(solution)/shard_map/all_to_all | solution.py:31
  100.7 9.6 %all-to-all-done.5 = bf16[32,1,64,128]{3,2,1,0:T(8,128)(2,1)S(1)} async-done(((bf16[32,1,64,128]{3,2,1,0:T(8,128)(2,1)}), bf16[32,1,64,128]{3,2,1,0:T(8,128)(2,1)S(1)}, u32[]{:S(2)}, u32[]{:S(2)}) %all-to-all-start.5) | async-done | bytes 524320 | tf_op jit(solution)/shard_map/all_to_all | solution.py:31
  110.3 8.3 %all-to-all-start.4 = ((bf16[32,1,64,128]{3,2,1,0:T(8,128)(2,1)}), bf16[32,1,64,128]{3,2,1,0:T(8,128)(2,1)}, u32[]{:S(2)}, u32[]{:S(2)}) async-start(bf16[32,1,64,128]{3,2,1,0:T(8,128)(2,1)} %copy.69), calls=%async_computation.4 | async-start | bytes 1048576 | tf_op jit(solution)/shard_map/all_to_all | solution.py:31
  121.8 6.5 all-to-all-done.4
  157.2 4.0 fusion.8
  164.9 4.5 fusion.4
  169.4 211.5 %all-gather.2.cloned.1.call-done = bf16[2,4096,2048]{2,1,0:T(8,128)(2,1)} async-done(((bf16[2,32,2048]{2,1,0:T(8,128)(2,1)}), bf16[2,4096,2048]{2,1,0:T(8,128)(2,1)}) %all-gather.2.cloned.1.call-update) | async-done | bytes 33554448 | tf_op jit(solution)/shard_map/all_gather | solution.py:157
  380.8 12.4 %fusion = bf16[128,4096]{1,0:T(8,128)(2,1)} fusion(bf16[2,4096,2048]{2,1,0:T(8,128)(2,1)} %all-gather.2.cloned.1.call-done, bf16[1,128,2048]{2,1,0:T(8,128)(2,1)S(1)} %copy-done), kind=kOutput, calls=%fused_computation.2 | convolution fusion | flops 2147483648 | bytes 18350080 | tf_op jit(solution)/shard_map/dot_general | solution.py:125
  393.2 11.6 %fusion.20 = bf16[1,128,4096]{2,1,0:T(8,128)(2,1)S(1)} fusion(bf16[128,4096]{1,0:T(8,128)(2,1)} %fusion, bf16[2,4096,2048]{2,1,0:T(8,128)(2,1)} %all-gather.2.cloned.1.call-done, pred[128]{0:T(512)(128)(4,1)S(1)} %compare_bitcast_fusion, bf16[1,128,2048]{2,1,0:T(8,128)(2,1)S(1)} %copy-done), kind=kOutput, calls=%fused_computation.42 | convolution fusion | flops 2148007936 | bytes 19398784 | tf_op jit(solution)/shard_map/dot_general | solution.py:125
  404.9 3.9 copy.75
  409.3 23.6 %reduce.73 = bf16[4096,128]{1,0:T(8,128)(2,1)S(1)} reduce(bf16[4096,1,128]{2,1,0:T(2,128)(2,1)} %bitcast.454, bf16[]{:T(256)} %broadcast.495), dimensions={1}, to_apply=%bitcast.334.reduce_sub_computation | reduce | bytes 2097154
  434.0 10.3 %all-to-all-start.7 = ((bf16[32,2,8192]{2,1,0:T(2,128)(2,1)}), bf16[32,2,8192]{2,1,0:T(2,128)(2,1)S(1)}, u32[]{:S(2)}, u32[]{:S(2)}) async-start(bf16[32,2,8192]{2,1,0:T(2,128)(2,1)} %reshape.1112), calls=%async_computation.7 | async-start | bytes 2097152 | tf_op jit(solution)/shard_map/all_to_all | solution.py:166
  444.3 4.6 constant_dynamic-update-slice_fusion.2
  448.9 5.0 constant_dynamic-update-slice_fusion.1
  455.8 4.3 copy.86
  460.2 24.4 %reduce.72 = bf16[4096,128]{1,0:T(8,128)(2,1)} reduce(bf16[4096,1,128]{2,1,0:T(2,128)(2,1)} %bitcast.455, bf16[]{:T(256)} %broadcast.495), dimensions={1}, to_apply=%bitcast.405.reduce_sub_computation | reduce | bytes 2097154
  486.7 9.9 %all-to-all-start.6 = ((bf16[32,2,8192]{2,1,0:T(2,128)(2,1)}), bf16[32,2,8192]{2,1,0:T(2,128)(2,1)}, u32[]{:S(2)}, u32[]{:S(2)}) async-start(bf16[32,2,8192]{2,1,0:T(2,128)(2,1)} %reshape.1110), calls=%async_computation.6 | async-start | bytes 2097152 | tf_op jit(solution)/shard_map/all_to_all | solution.py:155
  556.1 20.5 %copy.78 = bf16[3,4096,128]{2,0,1:T(4,128)(2,1)} copy(bf16[3,4096,128]{2,1,0:T(8,128)(2,1)S(1)} %pad_maximum_fusion) | data formatting | bytes 6291456 | tf_op jit(solution)/shard_map/concatenate | solution.py:37
  576.6 10.3 %all-to-all-start.8 = ((bf16[3,4096,128]{2,0,1:T(4,128)(2,1)}), bf16[3,4096,128]{2,0,1:T(4,128)(2,1)}, u32[]{:S(2)}, u32[]{:S(2)}) async-start(bf16[3,4096,128]{2,0,1:T(4,128)(2,1)} %copy.78), calls=%async_computation.8 | async-start | bytes 8388608 | tf_op jit(solution)/shard_map/all_to_all | solution.py:38
  586.9 4.3 reshape.1111
  593.9 8.1 %fusion.1 = bf16[128,2048]{1,0:T(8,128)(2,1)S(1)} fusion(bf16[128,4096]{0,1:T(8,128)(2,1)S(1)} %bitcast.493, bf16[2,4096,2048]{2,1,0:T(8,128)(2,1)} %all-gather.2.cloned.1.call-done), kind=kOutput, calls=%fused_computation.3 | convolution fusion | flops 2147483648 | bytes 18350080 | tf_op jit(solution)/shard_map/dot_general | solution.py:159
  602.1 8.9 %fusion.49 = bf16[1,128,2048]{2,1,0:T(8,128)(2,1)} fusion(bf16[128,2048]{1,0:T(8,128)(2,1)S(1)} %fusion.1, bf16[128,4096]{0,1:T(8,128)(2,1)S(1)} %bitcast.494, bf16[2,4096,2048]{2,1,0:T(8,128)(2,1)} %all-gather.2.cloned.1.call-done, pred[128]{0:T(512)(128)(4,1)S(1)} %copy-done.29), kind=kOutput, calls=%fused_computation.88 | convolution fusion | flops 2147745792 | bytes 18874496 | tf_op jit(solution)/shard_map/dot_general | solution.py:158
  611.0 35.8 %all-to-all-done.8 = bf16[3,4096,128]{2,0,1:T(4,128)(2,1)} async-done(((bf16[3,4096,128]{2,0,1:T(4,128)(2,1)}), bf16[3,4096,128]{2,0,1:T(4,128)(2,1)}, u32[]{:S(2)}, u32[]{:S(2)}) %all-to-all-start.8) | async-done | bytes 3145760 | tf_op jit(solution)/shard_map/all_to_all | solution.py:38
  646.7 10.9 %fusion.163 = (bf16[1,128,32,128]{3,0,1,2:T(2,128)(2,1)S(1)}, bf16[1,128,32,128]{3,0,1,2:T(2,128)(2,1)}, bf16[1,128,32,128]{3,0,1,2:T(2,128)(2,1)S(1)}) fusion(bf16[3,128,32,128]{3,0,1,2:T(4,128)(2,1)} %bitcast.93), kind=kLoop, calls=%fused_computation.257 | loop fusion | bytes 6291456 | tf_op jit(solution)/shard_map/split | solution.py:39
  662.1 3.8 copy.80
  (188 shorter events, 138.7 us)
Async XLA Ops:
  7.2 373.7 %copy-start = (bf16[1,128,2048]{2,1,0:T(8,128)(2,1)S(1)}, bf16[1,128,2048]{2,1,0:T(8,128)(2,1)}, u32[]{:S(2)}) copy-start(bf16[1,128,2048]{2,1,0:T(8,128)(2,1)} %param.47) | copy-start | bytes 1572868
  7.2 373.7 %all-gather.2.cloned.1.call-start = ((), (), s32[]{:S(2)}) async-start(), calls=%async_computation.9 | async-start | bytes 33816576 | tf_op jit(solution)/shard_map/all_gather | solution.py:157
  13.4 23.5 %all-to-all-start.3 = ((bf16[32,1,64,128]{3,2,1,0:T(8,128)(2,1)}), bf16[32,1,64,128]{3,2,1,0:T(8,128)(2,1)S(1)}, u32[]{:S(2)}, u32[]{:S(2)}) async-start(bf16[32,1,64,128]{3,2,1,0:T(8,128)(2,1)} %copy.65), calls=%async_computation.3 | async-start | bytes 1048576 | tf_op jit(solution)/shard_map/all_to_all | solution.py:31
  36.8 19.3 %all-to-all-start.2 = ((bf16[32,1,64,128]{3,2,1,0:T(8,128)(2,1)}), bf16[32,1,64,128]{3,2,1,0:T(8,128)(2,1)}, u32[]{:S(2)}, u32[]{:S(2)}) async-start(bf16[32,1,64,128]{3,2,1,0:T(8,128)(2,1)} %copy.64), calls=%async_computation.2 | async-start | bytes 1048576 | tf_op jit(solution)/shard_map/all_to_all | solution.py:31
  56.1 18.8 %all-to-all-start.1 = ((bf16[32,1,64,128]{3,2,1,0:T(8,128)(2,1)}), bf16[32,1,64,128]{3,2,1,0:T(8,128)(2,1)S(1)}, u32[]{:S(2)}, u32[]{:S(2)}) async-start(bf16[32,1,64,128]{3,2,1,0:T(8,128)(2,1)} %copy.60), calls=%async_computation.1 | async-start | bytes 1048576 | tf_op jit(solution)/shard_map/all_to_all | solution.py:31
  75.7 17.1 %all-to-all-start = ((bf16[32,1,64,128]{3,2,1,0:T(8,128)(2,1)}), bf16[32,1,64,128]{3,2,1,0:T(8,128)(2,1)}, u32[]{:S(2)}, u32[]{:S(2)}) async-start(bf16[32,1,64,128]{3,2,1,0:T(8,128)(2,1)} %copy.59), calls=%async_computation | async-start | bytes 1048576 | tf_op jit(solution)/shard_map/all_to_all | solution.py:31
  86.4 32.1 %copy-start.27 = (s32[1,128]{1,0:T(1,128)S(1)}, s32[1,128]{1,0:T(1,128)}, u32[]{:S(2)}) copy-start(s32[1,128]{1,0:T(1,128)} %param.45) | copy-start | bytes 1540
  88.8 31.9 %copy-start.15 = (bf16[32,1,64,128]{3,2,1,0:T(8,128)(2,1)S(1)}, bf16[32,1,64,128]{3,2,1,0:T(8,128)(2,1)}, u32[]{:S(2)}) copy-start(bf16[32,1,64,128]{3,2,1,0:T(8,128)(2,1)} %copy-done.14) | copy-start | bytes 1572868
  92.8 17.5 %all-to-all-start.5 = ((bf16[32,1,64,128]{3,2,1,0:T(8,128)(2,1)}), bf16[32,1,64,128]{3,2,1,0:T(8,128)(2,1)S(1)}, u32[]{:S(2)}, u32[]{:S(2)}) async-start(bf16[32,1,64,128]{3,2,1,0:T(8,128)(2,1)} %copy.70), calls=%async_computation.5 | async-start | bytes 1048576 | tf_op jit(solution)/shard_map/all_to_all | solution.py:31
  110.3 18.1 %copy-start.16 = (bf16[32,1,64,128]{3,2,1,0:T(8,128)(2,1)}, bf16[32,1,64,128]{3,2,1,0:T(8,128)(2,1)S(1)}, u32[]{:S(2)}) copy-start(bf16[32,1,64,128]{3,2,1,0:T(8,128)(2,1)S(1)} %all-to-all-done.5) | copy-start | bytes 1572868
  110.3 18.1 %all-to-all-start.4 = ((bf16[32,1,64,128]{3,2,1,0:T(8,128)(2,1)}), bf16[32,1,64,128]{3,2,1,0:T(8,128)(2,1)}, u32[]{:S(2)}, u32[]{:S(2)}) async-start(bf16[32,1,64,128]{3,2,1,0:T(8,128)(2,1)} %copy.69), calls=%async_computation.4 | async-start | bytes 1048576 | tf_op jit(solution)/shard_map/all_to_all | solution.py:31
  118.6 274.7 %copy-start.28 = (pred[128]{0:T(512)(128)(4,1)}, pred[128]{0:T(512)(128)(4,1)S(1)}, u32[]{:S(2)}) copy-start(pred[128]{0:T(512)(128)(4,1)S(1)} %compare_bitcast_fusion) | copy-start | bytes 388
  121.8 32.1 %copy-start.7 = (bf16[32,1,128,128]{3,2,0,1:T(8,128)(2,1)}, bf16[32,1,128,128]{3,2,0,1:T(8,128)(2,1)S(1)}, u32[]{:S(2)}) copy-start(bf16[32,1,128,128]{3,2,0,1:T(8,128)(2,1)S(1)} %pad_maximum_fusion.1) | copy-start | bytes 3145732
  131.1 2.8 copy-start.19
  132.8 6.1 copy-start.12
  132.8 6.1 copy-start.23
  133.3 5.6 copy-start.25
  134.6 5.5 copy-start.10
  146.6 3.7 copy-start.2
  434.0 52.7 %all-to-all-start.7 = ((bf16[32,2,8192]{2,1,0:T(2,128)(2,1)}), bf16[32,2,8192]{2,1,0:T(2,128)(2,1)S(1)}, u32[]{:S(2)}, u32[]{:S(2)}) async-start(bf16[32,2,8192]{2,1,0:T(2,128)(2,1)} %reshape.1112), calls=%async_computation.7 | async-start | bytes 2097152 | tf_op jit(solution)/shard_map/all_to_all | solution.py:166
  444.3 9.6 %slice-start = ((s8[8388608]{0:T(1024)(128)(4,1)}), s8[4194304]{0:T(1024)(128)(4,1)S(1)}, s32[]{:S(2)}) async-start(s8[8388608]{0:T(1024)(128)(4,1)} %bitcast.406), calls=%async_computation.10 | async-start | bytes 8388608
  448.9 5.0 slice-start.1
  486.7 89.9 %all-to-all-start.6 = ((bf16[32,2,8192]{2,1,0:T(2,128)(2,1)}), bf16[32,2,8192]{2,1,0:T(2,128)(2,1)}, u32[]{:S(2)}, u32[]{:S(2)}) async-start(bf16[32,2,8192]{2,1,0:T(2,128)(2,1)} %reshape.1110), calls=%async_computation.6 | async-start | bytes 2097152 | tf_op jit(solution)/shard_map/all_to_all | solution.py:155
  505.1 3.3 copy-start.8
  511.0 5.2 slice-start.8
  512.9 3.4 slice-start.9
  512.9 4.5 slice-start.6
  516.2 2.7 slice-start.4
  528.3 4.0 slice-start.2
  576.6 70.2 %all-to-all-start.8 = ((bf16[3,4096,128]{2,0,1:T(4,128)(2,1)}), bf16[3,4096,128]{2,0,1:T(4,128)(2,1)}, u32[]{:S(2)}, u32[]{:S(2)}) async-start(bf16[3,4096,128]{2,0,1:T(4,128)(2,1)} %copy.78), calls=%async_computation.8 | async-start | bytes 8388608 | tf_op jit(solution)/shard_map/all_to_all | solution.py:38
  593.9 8.1 %copy-start.29 = (pred[128]{0:T(512)(128)(4,1)S(1)}, pred[128]{0:T(512)(128)(4,1)}, u32[]{:S(2)}) copy-start(pred[128]{0:T(512)(128)(4,1)} %copy-done.28) | copy-start | bytes 388
  665.9 6.8 %copy-start.1 = (bf16[1,128,2048]{2,1,0:T(8,128)(2,1)S(1)}, bf16[1,128,2048]{2,1,0:T(8,128)(2,1)}, u32[]{:S(2)}) copy-start(bf16[1,128,2048]{2,1,0:T(8,128)(2,1)} %param.47) | copy-start | bytes 1572868
  (18 other events, 36.9 us)
Sparse Core Ops, SparseCore 0:
  9.7 371.0 all-gather.1
where the time goes:
time: 687 us; the launch traced here: 680 us
  waiting for transfers between devices  295 us (43%)
  matrix products  112 us (16%)
  local copies, waits for them, and re-layouts  102 us (15%)
  starting transfers between devices  80 us (12%)
  other arithmetic  76.6 us (11%)
  between operations  15.2 us (2%)
    all_gather x1, waiting for transfers between devices, per_device(): lax.all_gather(out_weight, ('fsdp', 'ctx'), axis=1, tiled=True)  211 us
    all_to_all x6, starting transfers between devices, exchange_in_pieces(): lax.all_to_all(share, axis, split_axis=0, concat_axis=0, tiled=True)  49.5 us
    unnamed x7, other arithmetic  48 us
    all_to_all x6, waiting for transfers between devices, exchange_in_pieces(): lax.all_to_all(share, axis, split_axis=0, concat_axis=0, tiled=True)  46.9 us
    all_to_all x1, waiting for transfers between devices, sent_together(): lax.all_to_all(both, axis, split_axis=split_dim, concat_axis=concat_dim,...  35.8 us
    unnamed x90, local copies, waits for them, and re-layouts  28.1 us
    split x7, local copies, waits for them, and re-layouts, sent_together(): jnp.split(filled, [sum(widths[:k]) for k in range(1, len(widths))], axis=...  26 us
    dot_general x2, matrix products, transposed_product(): lax.dot_general(left, right, (((1,), (1,)), ((), ())), preferred_element_...  24 us
  transfers between devices with their start and end apart: 10, of which 8 were waited for; matrix products, arithmetic and copies ran while one was open for 30% of the time, Pallas kernels for 0%

commit v1 on v0

--- a/solution.py
+++ b/solution.py
@@ -154,7 +154,12 @@
     sending = heads_last(attention, length, local_width)
     attn_rows = lax.all_to_all(sending, "ctx", split_axis=1, concat_axis=2, tiled=True)[0]
     upstream = grad_projected[0]
-    weight_piece = lax.all_gather(out_weight, ("fsdp", "ctx"), axis=1, tiled=True)
+    weight_piece = jnp.concatenate(
+        lax.all_to_all(
+            jnp.stack([out_weight] * lax.axis_size(("fsdp", "ctx"))), ("fsdp", "ctx"), 0, 0
+        ),
+        axis=1,
+    )
     text_out = jnp.dot(attn_rows, weight_piece[0], preferred_element_type=jnp.float32)
     image_out = jnp.dot(attn_rows, weight_piece[1], preferred_element_type=jnp.float32)
     text_grad = transposed_product(upstream, weight_piece[0])

time: 687 us -> 1020 us (1.48)
  waiting for transfers between devices: 295 us -> 563 us
  local copies, waits for them, and re-layouts: 102 us -> 137 us
  starting transfers between devices: 80 us -> 103 us
  blocking collectives: 0 us -> 15.8 us
  between operations: 15.2 us -> 1.87 us
    all_to_all x0 -> x1, waiting for transfers between devices: none -> 496 us  [per_device(): lax.all_to_all(jnp.stack([out_weight] * lax.axis_size(('fsdp', 'ctx'))),...]
    all_gather x1 -> x0, waiting for transfers between devices: 211 us -> none  [per_device(): lax.all_gather(out_weight, ('fsdp', 'ctx'), axis=1, tiled=True)]
    slice x0 -> x1, local copies, waits for them, and re-layouts: none -> 23.8 us  [per_device(): weight_piece[0]]
    all_to_all x1, starting transfers between devices: 10.3 us -> 32.8 us  [per_device(): lax.all_to_all(grad_rows[None], 'ctx', split_axis=2, concat_axis=1, tiled...]
    all_to_all x6 -> x5, waiting for transfers between devices: 46.9 us -> 30.2 us  [exchange_in_pieces(): lax.all_to_all(share, axis, split_axis=0, concat_axis=0, tiled=True)]
    all_to_all x0 -> x1, blocking collectives: none -> 15.8 us  [exchange_in_pieces(): lax.all_to_all(share, axis, split_axis=0, concat_axis=0, tiled=True)]
    another operation x0 -> x1, local copies, waits for them, and re-layouts: none -> 11 us  [per_device(): jnp.stack([out_weight] * lax.axis_size(('fsdp', 'ctx')))]
    all_to_all x6 -> x5, starting transfers between devices: 49.5 us -> 41.4 us  [exchange_in_pieces(): lax.all_to_all(share, axis, split_axis=0, concat_axis=0, tiled=True)]
  transfers between devices with their start and end apart: 10 -> 9, of which waited for: 8 -> 7; matrix products, arithmetic and copies ran while one was open for 30% -> 20% of each run, Pallas kernels for 0% -> 0%
where the time goes in v1:
time: 1020 us; the launch traced here: 1010 us
  waiting for transfers between devices  563 us (55%)
  local copies, waits for them, and re-layouts  137 us (13%)
  matrix products  118 us (12%)
  starting transfers between devices  103 us (10%)
  other arithmetic  74.4 us (7%)
  blocking collectives  15.8 us (2%)
    all_to_all x1, waiting for transfers between devices, per_device(): lax.all_to_all(jnp.stack([out_weight] * lax.axis_size(('fsdp', 'ctx'))),...  496 us
    unnamed x7, other arithmetic  47.8 us
    all_to_all x5, starting transfers between devices, exchange_in_pieces(): lax.all_to_all(share, axis, split_axis=0, concat_axis=0, tiled=True)  41.4 us
    all_to_all x1, waiting for transfers between devices, sent_together(): lax.all_to_all(both, axis, split_axis=split_dim, concat_axis=concat_dim,...  36.6 us
    all_to_all x1, starting transfers between devices, per_device(): lax.all_to_all(grad_rows[None], 'ctx', split_axis=2, concat_axis=1, tiled...  32.8 us
    all_to_all x5, waiting for transfers between devices, exchange_in_pieces(): lax.all_to_all(share, axis, split_axis=0, concat_axis=0, tiled=True)  30.2 us
    unnamed x104, local copies, waits for them, and re-layouts  28.2 us
    split x7, local copies, waits for them, and re-layouts, sent_together(): jnp.split(filled, [sum(widths[:k]) for k in range(1, len(widths))], axis=...  26 us
  transfers between devices with their start and end apart: 9, of which 7 were waited for; matrix products, arithmetic and copies ran while one was open for 20% of the time, Pallas kernels for 0%

profile of v1, /device:TPU:18, one launch (start us, length us, event | category | flops | bytes accessed | tf_op | source)
XLA Modules:
  0.0 1013.5 jit_solution(1876662461089046674)
XLA Ops:
  6.1 10.9 %all-to-all-start = ((bf16[32,1,64,128]{3,2,1,0:T(8,128)(2,1)}), bf16[32,1,64,128]{3,2,1,0:T(8,128)(2,1)S(1)}, u32[]{:S(2)}, u32[]{:S(2)}) async-start(bf16[32,1,64,128]{3,2,1,0:T(8,128)(2,1)} %copy.59), calls=%async_computation | async-start | bytes 1048576 | tf_op jit(solution)/shard_map/all_to_all | solution.py:31
  18.1 8.7 all-to-all-done
  26.8 7.8 all-to-all-start.1
  43.1 7.5 all-to-all-start.2
  51.8 7.3 all-to-all-done.2
  59.8 7.8 all-to-all-start.3
  76.1 7.5 all-to-all-start.4
  84.0 8.0 all-to-all-done.4
  92.0 15.8 %all_to_all.83 = bf16[32,1,64,128]{3,2,1,0:T(8,128)(2,1)} all-to-all(bf16[32,1,64,128]{3,2,1,0:T(8,128)(2,1)S(1)} %copy.70), channel_id=1, replica_groups=mesh['fsdp'=4,'ctx'=32] {'ctx'}, dimensions={0} | all-to-all | bytes 1048576 | tf_op jit(solution)/shard_map/all_to_all | solution.py:31
  107.8 11.0 %stack.2 = bf16[128,2,32,2048]{3,2,1,0:T(8,128)(2,1)} broadcast(bf16[2,32,2048]{2,1,0:T(8,128)(2,1)S(1)} %copy-done.29), dimensions={1,2,3} | broadcast | bytes 33816576 | tf_op jit(solution)/shard_map/stack | solution.py:159
  118.8 8.9 all-to-all-start.7
  155.6 3.9 fusion.4
  163.3 4.0 fusion
  167.4 495.9 %all-to-all-done.7 = bf16[128,2,32,2048]{3,2,1,0:T(8,128)(2,1)} async-done(((bf16[128,2,32,2048]{3,2,1,0:T(8,128)(2,1)}), bf16[128,2,32,2048]{3,2,1,0:T(8,128)(2,1)}, u32[]{:S(2)}, u32[]{:S(2)}) %all-to-all-start.7) | async-done | bytes 33554464 | tf_op jit(solution)/shard_map/all_to_all | solution.py:158
  663.3 23.8 %fusion.158 = (bf16[1,128,32,2048]{3,2,0,1:T(8,128)(2,1)}, bf16[1,128,32,2048]{3,2,0,1:T(8,128)(2,1)}) fusion(bf16[2,128,32,2048]{3,2,0,1:T(8,128)(2,1)} %bitcast.53), kind=kLoop, calls=%fused_computation.252 | loop fusion | bytes 67108864 | tf_op jit(solution)/shard_map/slice | solution.py:163
  687.1 11.4 %fusion.117 = bf16[128,4096]{1,0:T(8,128)(2,1)S(1)} fusion(bf16[4096,2048]{1,0:T(8,128)(2,1)} %bitcast.393, bf16[1,128,2048]{2,1,0:T(8,128)(2,1)S(1)} %copy-done), kind=kOutput, calls=%fused_computation.177 | convolution fusion | flops 2147483648 | bytes 18350080 | tf_op jit(solution)/shard_map/dot_general | solution.py:125
  698.5 12.3 %fusion.15 = bf16[1,128,4096]{2,1,0:T(8,128)(2,1)} fusion(bf16[128,4096]{1,0:T(8,128)(2,1)S(1)} %fusion.117, bf16[4096,2048]{1,0:T(8,128)(2,1)} %bitcast.395, pred[128]{0:T(512)(128)(4,1)} %compare_bitcast_fusion, bf16[1,128,2048]{2,1,0:T(8,128)(2,1)S(1)} %copy-done), kind=kOutput, calls=%fused_computation.36 | convolution fusion | flops 2148007936 | bytes 19398784 | tf_op jit(solution)/shard_map/dot_general | solution.py:125
  710.8 5.5 copy.75
  716.9 23.4 %reduce.73 = bf16[4096,128]{1,0:T(8,128)(2,1)S(1)} reduce(bf16[4096,1,128]{2,1,0:T(2,128)(2,1)} %bitcast.447, bf16[]{:T(256)} %broadcast.497), dimensions={1}, to_apply=%bitcast.317.reduce_sub_computation | reduce | bytes 2097154
  741.4 32.8 %all-to-all-start.8 = ((bf16[32,2,8192]{2,1,0:T(2,128)(2,1)}), bf16[32,2,8192]{2,1,0:T(2,128)(2,1)S(1)}, u32[]{:S(2)}, u32[]{:S(2)}) async-start(bf16[32,2,8192]{2,1,0:T(2,128)(2,1)} %reshape.1123), calls=%async_computation.8 | async-start | bytes 2097152 | tf_op jit(solution)/shard_map/all_to_all | solution.py:171
  774.2 4.6 constant_dynamic-update-slice_fusion.2
  778.8 5.0 constant_dynamic-update-slice_fusion.1
  785.7 4.4 copy.86
  790.1 24.4 %reduce.72 = bf16[4096,128]{1,0:T(8,128)(2,1)} reduce(bf16[4096,1,128]{2,1,0:T(2,128)(2,1)} %bitcast.448, bf16[]{:T(256)} %broadcast.497), dimensions={1}, to_apply=%bitcast.392.reduce_sub_computation | reduce | bytes 2097154
  816.6 9.9 all-to-all-start.6
  895.4 20.5 %copy.78 = bf16[3,4096,128]{2,0,1:T(4,128)(2,1)} copy(bf16[3,4096,128]{2,1,0:T(8,128)(2,1)S(1)} %pad_maximum_fusion) | data formatting | bytes 6291456 | tf_op jit(solution)/shard_map/concatenate | solution.py:37
  916.0 10.3 %all-to-all-start.9 = ((bf16[3,4096,128]{2,0,1:T(4,128)(2,1)}), bf16[3,4096,128]{2,0,1:T(4,128)(2,1)}, u32[]{:S(2)}, u32[]{:S(2)}) async-start(bf16[3,4096,128]{2,0,1:T(4,128)(2,1)} %copy.78), calls=%async_computation.9 | async-start | bytes 8388608 | tf_op jit(solution)/shard_map/all_to_all | solution.py:38
  926.2 4.3 reshape.1122
  933.3 8.1 fusion.171
  941.4 8.9 fusion.43
  950.4 36.6 %all-to-all-done.9 = bf16[3,4096,128]{2,0,1:T(4,128)(2,1)} async-done(((bf16[3,4096,128]{2,0,1:T(4,128)(2,1)}), bf16[3,4096,128]{2,0,1:T(4,128)(2,1)}, u32[]{:S(2)}, u32[]{:S(2)}) %all-to-all-start.9) | async-done | bytes 3145760 | tf_op jit(solution)/shard_map/all_to_all | solution.py:38
  987.0 10.9 %fusion.159 = (bf16[1,128,32,128]{3,0,1,2:T(2,128)(2,1)S(1)}, bf16[1,128,32,128]{3,0,1,2:T(2,128)(2,1)}, bf16[1,128,32,128]{3,0,1,2:T(2,128)(2,1)S(1)}) fusion(bf16[3,128,32,128]{3,0,1,2:T(4,128)(2,1)} %bitcast.94), kind=kLoop, calls=%fused_computation.253 | loop fusion | bytes 6291456 | tf_op jit(solution)/shard_map/split | solution.py:39
  (202 shorter events, 149.5 us)
Async XLA Ops:
  0.6 686.5 %copy-start = (bf16[1,128,2048]{2,1,0:T(8,128)(2,1)S(1)}, bf16[1,128,2048]{2,1,0:T(8,128)(2,1)}, u32[]{:S(2)}) copy-start(bf16[1,128,2048]{2,1,0:T(8,128)(2,1)} %param.47) | copy-start | bytes 1572868
  6.1 20.7 %all-to-all-start = ((bf16[32,1,64,128]{3,2,1,0:T(8,128)(2,1)}), bf16[32,1,64,128]{3,2,1,0:T(8,128)(2,1)S(1)}, u32[]{:S(2)}, u32[]{:S(2)}) async-start(bf16[32,1,64,128]{3,2,1,0:T(8,128)(2,1)} %copy.59), calls=%async_computation | async-start | bytes 1048576 | tf_op jit(solution)/shard_map/all_to_all | solution.py:31
  26.8 16.4 %all-to-all-start.1 = ((bf16[32,1,64,128]{3,2,1,0:T(8,128)(2,1)}), bf16[32,1,64,128]{3,2,1,0:T(8,128)(2,1)}, u32[]{:S(2)}, u32[]{:S(2)}) async-start(bf16[32,1,64,128]{3,2,1,0:T(8,128)(2,1)} %copy.60), calls=%async_computation.1 | async-start | bytes 1048576 | tf_op jit(solution)/shard_map/all_to_all | solution.py:31
  43.1 15.9 %all-to-all-start.2 = ((bf16[32,1,64,128]{3,2,1,0:T(8,128)(2,1)}), bf16[32,1,64,128]{3,2,1,0:T(8,128)(2,1)S(1)}, u32[]{:S(2)}, u32[]{:S(2)}) async-start(bf16[32,1,64,128]{3,2,1,0:T(8,128)(2,1)} %copy.64), calls=%async_computation.2 | async-start | bytes 1048576 | tf_op jit(solution)/shard_map/all_to_all | solution.py:31
  59.8 16.3 %all-to-all-start.3 = ((bf16[32,1,64,128]{3,2,1,0:T(8,128)(2,1)}), bf16[32,1,64,128]{3,2,1,0:T(8,128)(2,1)}, u32[]{:S(2)}, u32[]{:S(2)}) async-start(bf16[32,1,64,128]{3,2,1,0:T(8,128)(2,1)} %copy.65), calls=%async_computation.3 | async-start | bytes 1048576 | tf_op jit(solution)/shard_map/all_to_all | solution.py:31
  70.6 37.2 %copy-start.29 = (bf16[2,32,2048]{2,1,0:T(8,128)(2,1)S(1)}, bf16[2,32,2048]{2,1,0:T(8,128)(2,1)}, u32[]{:S(2)}) copy-start(bf16[2,32,2048]{2,1,0:T(8,128)(2,1)} %param.46) | copy-start | bytes 786436
  76.1 15.9 %all-to-all-start.4 = ((bf16[32,1,64,128]{3,2,1,0:T(8,128)(2,1)}), bf16[32,1,64,128]{3,2,1,0:T(8,128)(2,1)S(1)}, u32[]{:S(2)}, u32[]{:S(2)}) async-start(bf16[32,1,64,128]{3,2,1,0:T(8,128)(2,1)} %copy.69), calls=%async_computation.4 | async-start | bytes 1048576 | tf_op jit(solution)/shard_map/all_to_all | solution.py:31
  92.0 26.8 %copy-start.21 = (bf16[32,1,64,128]{3,2,1,0:T(8,128)(2,1)}, bf16[32,1,64,128]{3,2,1,0:T(8,128)(2,1)S(1)}, u32[]{:S(2)}) copy-start(bf16[32,1,64,128]{3,2,1,0:T(8,128)(2,1)S(1)} %all-to-all-done.4) | copy-start | bytes 1572868
  118.8 9.0 copy-start.36
  118.8 10.7 %copy-start.20 = (bf16[32,1,64,128]{3,2,1,0:T(8,128)(2,1)S(1)}, bf16[32,1,64,128]{3,2,1,0:T(8,128)(2,1)}, u32[]{:S(2)}) copy-start(bf16[32,1,64,128]{3,2,1,0:T(8,128)(2,1)} %copy-done.19) | copy-start | bytes 1572868
  118.8 544.5 %all-to-all-start.7 = ((bf16[128,2,32,2048]{3,2,1,0:T(8,128)(2,1)}), bf16[128,2,32,2048]{3,2,1,0:T(8,128)(2,1)}, u32[]{:S(2)}, u32[]{:S(2)}) async-start(bf16[128,2,32,2048]{3,2,1,0:T(8,128)(2,1)} %stack.2), calls=%async_computation.7 | async-start | bytes 67108864 | tf_op jit(solution)/shard_map/all_to_all | solution.py:158
  129.5 22.9 %copy-start.11 = (bf16[32,1,128,128]{3,2,0,1:T(8,128)(2,1)}, bf16[32,1,128,128]{3,2,0,1:T(8,128)(2,1)S(1)}, u32[]{:S(2)}) copy-start(bf16[32,1,128,128]{3,2,0,1:T(8,128)(2,1)S(1)} %pad_maximum_fusion.1) | copy-start | bytes 3145732
  131.0 21.4 %copy-start.26 = (bf16[32,1,128,128]{3,2,0,1:T(8,128)(2,1)}, bf16[32,1,128,128]{3,2,0,1:T(8,128)(2,1)S(1)}, u32[]{:S(2)}) copy-start(bf16[32,1,128,128]{3,2,0,1:T(8,128)(2,1)S(1)} %pad_maximum_fusion.2) | copy-start | bytes 3145732
  132.2 6.1 copy-start.17
  132.2 6.1 copy-start.32
  132.8 5.6 copy-start.34
  134.1 5.5 copy-start.14
  741.4 75.2 %all-to-all-start.8 = ((bf16[32,2,8192]{2,1,0:T(2,128)(2,1)}), bf16[32,2,8192]{2,1,0:T(2,128)(2,1)S(1)}, u32[]{:S(2)}, u32[]{:S(2)}) async-start(bf16[32,2,8192]{2,1,0:T(2,128)(2,1)} %reshape.1123), calls=%async_computation.8 | async-start | bytes 2097152 | tf_op jit(solution)/shard_map/all_to_all | solution.py:171
  774.2 9.6 slice-start
  816.6 99.3 %all-to-all-start.6 = ((bf16[32,2,8192]{2,1,0:T(2,128)(2,1)}), bf16[32,2,8192]{2,1,0:T(2,128)(2,1)}, u32[]{:S(2)}, u32[]{:S(2)}) async-start(bf16[32,2,8192]{2,1,0:T(2,128)(2,1)} %reshape.1121), calls=%async_computation.6 | async-start | bytes 2097152 | tf_op jit(solution)/shard_map/all_to_all | solution.py:155
  836.3 5.2 copy-start.18
  836.3 5.2 copy-start.33
  836.3 5.2 copy-start.35
  841.5 7.3 slice-start.8
  843.7 5.1 slice-start.9
  843.7 7.4 slice-start.6
  846.7 7.1 slice-start.4
  848.8 5.0 slice-start.5
  851.1 5.6 slice-start.2
  916.0 71.1 %all-to-all-start.9 = ((bf16[3,4096,128]{2,0,1:T(4,128)(2,1)}), bf16[3,4096,128]{2,0,1:T(4,128)(2,1)}, u32[]{:S(2)}, u32[]{:S(2)}) async-start(bf16[3,4096,128]{2,0,1:T(4,128)(2,1)} %copy.78), calls=%async_computation.9 | async-start | bytes 8388608 | tf_op jit(solution)/shard_map/all_to_all | solution.py:38
  933.3 8.1 copy-start.31
  1006.2 6.8 copy-start.1
  (24 other events, 67.0 us)
